TPU v7x, 128 devices: a whole 4x4x4 slice. The times are simulated.
128 devices in a mesh: dp: 8 (over y, core), ctx: 16 (over z, x).
Axes of the slice: x: 4, y: 4, z: 4, core: 2. Of those that a mesh axis runs over, the one named last changes fastest.
Arguments:
- queries: bfloat16 [8, 4096, 256], P('dp', 'ctx'), may hold values from -6 to 6
- keys: bfloat16 [8, 4096, 256], P('dp', 'ctx'), may hold values from -6 to 6
- values: bfloat16 [8, 4096, 256], P('dp', 'ctx'), may hold values from -6 to 6
- grad_out: bfloat16 [8, 4096, 256], P('dp', 'ctx'), may hold values from -6 to 6
- log_norm: float32 [8, 2, 4096], P('dp', None, 'ctx'), may hold values from 5 to 7
- offsets: int32 [2, 5], replicated, may hold values from 0 to 15
- q_gain: float32 [256], replicated, may hold values from 0.5 to 2
Outputs:
- grad_queries: bfloat16 [8, 4096, 256], P('dp', 'ctx')
- grad_keys: bfloat16 [8, 4096, 256], P('dp', 'ctx')
- grad_values: bfloat16 [8, 4096, 256], P('dp', 'ctx')
- grad_gain: float32 [256], replicated
All inputs are finite; a program needn't handle non-finite values.
Results may differ from a plain program's by a relative error of at most 0.013.
The roundings to bfloat16 on the way count: a program that leaves them out, or rounds other values in their place, can miss the bound.
Values may be sent and summed in bfloat16 or wider, within the bound.
No kernel may reach another device: no remote copies, remote signals or barrier semaphores. Data moves between devices by JAX's collectives and lax.ppermute only.
A program may use at most 64 MiB of HBM per device.

v0:
```python
import math
import jax
import jax.numpy as jnp
from jax import lax
from jax.sharding import PartitionSpec as P

BLOCK = 128
LEVELS = 5


def swapped(block, axis, stride):
    count = lax.axis_size(axis)
    route = []
    for low in range(count):
        high = low | 1 << stride
        if high != low and high < count:
            route += [(low, high), (high, low)]
    return lax.ppermute(block, axis, route)


def slot_table(device_local, offset_vec, stride, block_count):
    slot_count = (block_count + stride - 1) // stride
    base_block = device_local * block_count + jnp.zeros_like(offset_vec)
    first_step = jnp.maximum((base_block - offset_vec + stride - 1) // stride, 0)
    step_index = first_step[..., None] + jnp.arange(slot_count, dtype=jnp.int32)
    global_block = offset_vec[..., None] + stride * step_index
    local_block = global_block - base_block[..., None]
    usable = (step_index < block_count) & (local_block >= 0) & (local_block < block_count)
    return (jnp.clip(local_block, 0, block_count - 1), usable.astype(jnp.float32))


def segment_slots(shift_vec, span_len, block_count):
    device_col = jnp.arange(span_len, dtype=jnp.int32)[:, None]
    seg_block, seg_usable = slot_table(device_col, shift_vec[None, :], span_len, block_count)
    return (seg_block.transpose(1, 0, 2), seg_usable.transpose(1, 0, 2))


def select_table(local_block, block_count):
    return (local_block[..., None] == jnp.arange(block_count, dtype=jnp.int32)).astype(jnp.float32)


def pick_blocks(data, table):
    head_count, block_count = (data.shape[0], data.shape[1])
    flat = data.reshape(head_count, block_count, -1).astype(jnp.float32)
    chosen = jnp.einsum(
        "hsb,hbx->hsx",
        table,
        flat,
        precision=lax.Precision.HIGHEST,
        preferred_element_type=jnp.float32,
    ).astype(data.dtype)
    return chosen.reshape((head_count, -1) + data.shape[3:])


def place_rows(accum, contrib, table, usable):
    head_count, block_count = (accum.shape[0], accum.shape[1])
    slot_count = table.shape[1]
    weights = table * usable[..., None]
    shaped = contrib.reshape(head_count, slot_count, -1)
    added = jnp.einsum(
        "hsb,hsx->hbx",
        weights,
        shaped,
        precision=lax.Precision.HIGHEST,
        preferred_element_type=jnp.float32,
    )
    return accum + added.reshape(accum.shape)


def attend(
    query_rows,
    dout_rows,
    norm_rows,
    query_mask,
    key_rows,
    value_rows,
    key_mask,
    score_scale,
    row_block,
):
    head_count, query_count, head_dim = query_rows.shape
    steps = query_count // row_block

    def split(array):
        return jnp.moveaxis(array.reshape((head_count, steps, row_block) + array.shape[2:]), 1, 0)

    def step_fn(carry, parts):
        query_blk, dout_blk, norm_blk, mask_blk = parts
        scores = (
            jnp.einsum("hqd,hkd->hqk", query_blk, key_rows, preferred_element_type=jnp.float32)
            * score_scale
        )
        probs = jnp.exp(scores - norm_blk[:, :, None]) * mask_blk[:, :, None] * key_mask[:, None, :]
        probs_low = probs.astype(jnp.bfloat16)
        prob_grad = jnp.einsum(
            "hqd,hkd->hqk", dout_blk, value_rows, preferred_element_type=jnp.float32
        )
        dscore = (probs * prob_grad).astype(jnp.bfloat16)
        query_grad = (
            jnp.einsum("hqk,hkd->hqd", dscore, key_rows, preferred_element_type=jnp.float32)
            * score_scale
        )
        key_part = (
            jnp.einsum("hqk,hqd->hkd", dscore, query_blk, preferred_element_type=jnp.float32)
            * score_scale
        )
        value_part = jnp.einsum(
            "hqk,hqd->hkd", probs_low, dout_blk, preferred_element_type=jnp.float32
        )
        return ((carry[0] + key_part, carry[1] + value_part), query_grad)

    start = jnp.zeros((head_count, key_rows.shape[1], head_dim), jnp.float32)
    totals, query_parts = lax.scan(
        step_fn,
        (start, start),
        (split(query_rows), split(dout_rows), split(norm_rows), split(query_mask)),
    )
    query_grad = jnp.moveaxis(query_parts, 0, 1).reshape(head_count, query_count, head_dim)
    return (query_grad, totals[0], totals[1])


def swap_up(payload, my_index, bit_total):
    for bit_idx in range(bit_total):
        partner = swapped(payload, "ctx", bit_idx)
        lower_half = my_index >> bit_idx & 1 == 0
        payload = jnp.where(
            lower_half,
            jnp.concatenate([payload, partner], axis=1),
            jnp.concatenate([partner, payload], axis=1),
        )
    return payload


def swap_down(sums_kv, my_index, bit_total):
    head_count = sums_kv.shape[0]
    for bit_idx in reversed(range(bit_total)):
        halves = sums_kv.reshape(head_count, 2, -1, sums_kv.shape[-1])
        lower_half = my_index >> bit_idx & 1 == 0
        kept_half = jnp.where(lower_half, halves[:, 0], halves[:, 1])
        sent_half = jnp.where(lower_half, halves[:, 1], halves[:, 0])
        sums_kv = kept_half + swapped(sent_half.astype(jnp.bfloat16), "ctx", bit_idx).astype(
            sent_half.dtype
        )
    return sums_kv


def body(queries, keys, values, grad_out, log_norm, offsets, q_gain):
    query_raw = queries[0]
    token_count, proj_width = query_raw.shape
    head_count = log_norm.shape[1]
    head_dim = proj_width // head_count
    block_count = token_count // BLOCK
    ctx_size = lax.axis_size("ctx")
    score_scale = head_dim ** (-0.5)
    scaled = (query_raw.astype(jnp.float32) * q_gain).astype(jnp.bfloat16)

    def heads(matrix):
        return (
            matrix.reshape(token_count, head_count, head_dim)
            .transpose(1, 0, 2)
            .reshape(head_count, block_count, BLOCK, head_dim)
        )

    query_all = heads(scaled)
    key_all = heads(keys[0])
    value_all = heads(values[0])
    dout_all = heads(grad_out[0])
    norm_all = log_norm[0].reshape(head_count, block_count, BLOCK)
    query_acc = jnp.zeros((head_count, block_count, BLOCK, head_dim), jnp.float32)
    kv_acc = jnp.zeros((head_count, block_count, BLOCK, 2 * head_dim), jnp.float32)
    my_index = lax.axis_index("ctx")
    for level_idx in range(LEVELS):
        span_len = min(2**level_idx, ctx_size)
        shift_vec = offsets[:, level_idx] % span_len
        local_block, usable = slot_table(my_index % span_len, shift_vec, span_len, block_count)
        table = select_table(local_block, block_count)
        slot_count = local_block.shape[1]
        row_block = BLOCK * math.gcd(slot_count, max(1, 512 // BLOCK))
        query_own = pick_blocks(query_all, table)
        dout_own = pick_blocks(dout_all, table)
        norm_own = pick_blocks(norm_all, table)
        mask_own = jnp.repeat(usable, BLOCK, axis=1)
        payload = jnp.concatenate(
            [pick_blocks(key_all, table), pick_blocks(value_all, table)], axis=2
        )
        bit_total = span_len.bit_length() - 1
        payload = swap_up(payload, my_index, bit_total)
        seg_block, seg_usable = segment_slots(shift_vec, span_len, block_count)
        seg_mask = jnp.repeat(seg_usable.reshape(head_count, -1), BLOCK, axis=1)
        level_query, level_key, level_value = attend(
            query_own,
            dout_own,
            norm_own,
            mask_own,
            payload[..., :head_dim],
            payload[..., head_dim:],
            seg_mask,
            score_scale,
            row_block,
        )
        sums_kv = jnp.concatenate([level_key, level_value], axis=2)
        sums_kv = swap_down(sums_kv, my_index, bit_total)
        query_acc = place_rows(query_acc, level_query, table, usable)
        kv_acc = place_rows(kv_acc, sums_kv, table, usable)

    def to_rows(field_acc):
        return (
            field_acc.reshape(head_count, token_count, -1)
            .transpose(1, 0, 2)
            .reshape(token_count, -1)
        )

    dq_rows = to_rows(query_acc)
    grad_queries = (dq_rows * q_gain).astype(jnp.bfloat16)
    grad_keys = to_rows(kv_acc[..., :head_dim]).astype(jnp.bfloat16)
    grad_values = to_rows(kv_acc[..., head_dim:]).astype(jnp.bfloat16)
    gain_total = lax.psum(jnp.sum(query_raw.astype(jnp.float32) * dq_rows, axis=0), ("dp", "ctx"))
    return (grad_queries[None], grad_keys[None], grad_values[None], gain_total)


def solution(mesh):
    in_specs = (
        P("dp", "ctx", None),
        P("dp", "ctx", None),
        P("dp", "ctx", None),
        P("dp", "ctx", None),
        P("dp", None, "ctx"),
        P(),
        P(),
    )
    out_specs = (P("dp", "ctx", None), P("dp", "ctx", None), P("dp", "ctx", None), P())
    return jax.shard_map(body, mesh=mesh, in_specs=in_specs, out_specs=out_specs, check_vma=False)
```

profile of v0, /device:TPU:0, one launch (start us, length us, event | category | flops | bytes accessed | tf_op | source)
XLA Modules:
  0.0 272.5 jit_solution(3529592541120777040)
XLA Ops:
  1.7 1.7 clamp_reduce_fusion.3
  34.6 3.2 %collective-permute-start.2 = (bf16[2,256,256]{2,1,0:T(8,128)(2,1)S(1)}, bf16[2,256,256]{2,1,0:T(8,128)(2,1)S(1)}, u32[]{:S(2)}, u32[]{:S(2)}) collective-permute-start(bf16[2,256,256]{2,1,0:T(8,128)(2,1)S(1)} %maximum_select_fusion.7), channel_id=1, source_target_pairs={{0,2},{2,0},{1,3},{3,1},{4,6},{6,4},{5,7},{7,5},{8,10},{10,8},{9,1... | collective-permute-start | bytes 786440 | tf_op jit(solution)/shard_map/ppermute | solution.py:18
  40.1 2.0 collective-permute-start.7
  47.9 9.2 %collective-permute-done.4 = bf16[2,256,256]{2,1,0:T(8,128)(2,1)} collective-permute-done((bf16[2,256,256]{2,1,0:T(8,128)(2,1)}, bf16[2,256,256]{2,1,0:T(8,128)(2,1)}, u32[]{:S(2)}, u32[]{:S(2)}) %collective-permute-start.4) | collective-permute-done | bytes 262176 | tf_op jit(solution)/shard_map/ppermute | solution.py:18
  58.4 2.4 collective-permute-start.5
  63.1 3.0 %collective-permute-start.11 = (bf16[2,256,256]{2,1,0:T(8,128)(2,1)}, bf16[2,256,256]{2,1,0:T(8,128)(2,1)}, u32[]{:S(2)}, u32[]{:S(2)}) collective-permute-start(bf16[2,256,256]{2,1,0:T(8,128)(2,1)} %fusion.49), channel_id=1, source_target_pairs={{0,2},{2,0},{1,3},{3,1},{4,6},{6,4},{5,7},{7,5},{8,10},{10,8},{9,1... | collective-permute-start | bytes 786440 | tf_op jit(solution)/shard_map/ppermute | solution.py:18
  66.1 2.2 maximum_select_fusion.5
  68.4 4.8 %collective-permute-done.5 = bf16[2,512,256]{2,1,0:T(8,128)(2,1)} collective-permute-done((bf16[2,512,256]{2,1,0:T(8,128)(2,1)S(1)}, bf16[2,512,256]{2,1,0:T(8,128)(2,1)}, u32[]{:S(2)}, u32[]{:S(2)}) %collective-permute-start.5) | collective-permute-done | bytes 524320 | tf_op jit(solution)/shard_map/ppermute | solution.py:18
  78.5 3.0 %reshape.1673 = f32[2,2,512,256]{2,1,3,0:T(2,128)S(1)} reshape(f32[2,1024,256]{1,2,0:T(8,128)} %pad_maximum_fusion.1) | data formatting | bytes 4194304 | tf_op jit(solution)/shard_map/reshape | solution.py:137
  81.6 2.9 %fusion.212 = (f32[2,1,512,256]{2,1,3,0:T(1,128)}, f32[2,1,512,256]{2,1,3,0:T(1,128)}) fusion(f32[2,2,512,256]{2,1,3,0:T(2,128)S(1)} %reshape.1673), kind=kLoop, calls=%fused_computation.413 | loop fusion | bytes 4194304 | tf_op jit(solution)/shard_map/slice | solution.py:139
  84.5 2.3 copy.151
  86.9 2.4 copy.152
  89.4 2.7 collective-permute-start.13
  92.1 1.8 maximum_select_fusion.2
  93.8 3.7 %collective-permute-start.9 = (bf16[2,1024,256]{2,1,0:T(8,128)(2,1)S(1)}, bf16[2,1024,256]{2,1,0:T(8,128)(2,1)S(1)}, u32[]{:S(2)}, u32[]{:S(2)}) collective-permute-start(bf16[2,1024,256]{2,1,0:T(8,128)(2,1)S(1)} %maximum_select_fusion.2), channel_id=1, source_target_pairs={{0,8},{8,0},{1,9},{9,1},{2,10},{10,2},{3,11},{11,3},{4,12},{12,4},... | collective-permute-start | bytes 3145736 | tf_op jit(solution)/shard_map/ppermute | solution.py:18
  101.1 1.7 collective-permute-start.12
  102.8 2.1 collective-permute-done.13
  105.2 18.4 %collective-permute-done.9 = bf16[2,1024,256]{2,1,0:T(8,128)(2,1)S(1)} collective-permute-done((bf16[2,1024,256]{2,1,0:T(8,128)(2,1)S(1)}, bf16[2,1024,256]{2,1,0:T(8,128)(2,1)S(1)}, u32[]{:S(2)}, u32[]{:S(2)}) %collective-permute-start.9) | collective-permute-done | bytes 1048608 | tf_op jit(solution)/shard_map/ppermute | solution.py:18
  127.4 2.5 pad_maximum_fusion
  129.9 6.6 %reshape.1677 = f32[2,2,1024,256]{2,1,3,0:T(2,128)} reshape(f32[2,2048,256]{1,2,0:T(8,128)} %pad_maximum_fusion) | data formatting | bytes 8388608 | tf_op jit(solution)/shard_map/reshape | solution.py:137
  136.5 9.1 %fusion.211 = (f32[2,1,1024,256]{2,1,3,0:T(1,128)}, f32[2,1,1024,256]{2,1,3,0:T(1,128)}) fusion(f32[2,2,1024,256]{2,1,3,0:T(2,128)} %reshape.1677), kind=kLoop, calls=%fused_computation.412 | loop fusion | bytes 8388608 | tf_op jit(solution)/shard_map/slice | solution.py:139
  145.6 4.6 %copy.157 = f32[2,1,1024,256]{3,2,0,1:T(8,128)S(1)} copy(f32[2,1,1024,256]{2,1,3,0:T(1,128)} %get-tuple-element.141) | data formatting | bytes 4194304
  150.2 6.0 %copy.158 = f32[2,1,1024,256]{3,2,0,1:T(8,128)} copy(f32[2,1,1024,256]{2,1,3,0:T(1,128)} %get-tuple-element.142) | data formatting | bytes 4194304
  156.2 1.9 fusion.36
  158.3 3.1 %collective-permute-start.14 = (bf16[2,256,256]{2,1,0:T(8,128)(2,1)S(1)}, bf16[2,256,256]{2,1,0:T(8,128)(2,1)S(1)}, u32[]{:S(2)}, u32[]{:S(2)}) collective-permute-start(bf16[2,256,256]{2,1,0:T(8,128)(2,1)S(1)} %fusion.50), channel_id=1, source_target_pairs={{0,2},{2,0},{1,3},{3,1},{4,6},{6,4},{5,7},{7,5},{8,10},{10,8},{9,1... | collective-permute-start | bytes 786440 | tf_op jit(solution)/shard_map/ppermute | solution.py:18
  163.7 3.3 %collective-permute-done.14 = bf16[2,256,256]{2,1,0:T(8,128)(2,1)S(1)} collective-permute-done((bf16[2,256,256]{2,1,0:T(8,128)(2,1)S(1)}, bf16[2,256,256]{2,1,0:T(8,128)(2,1)S(1)}, u32[]{:S(2)}, u32[]{:S(2)}) %collective-permute-start.14) | collective-permute-done | bytes 262176 | tf_op jit(solution)/shard_map/ppermute | solution.py:18
  167.9 14.9 %collective-permute-done.16 = bf16[2,1024,256]{2,1,0:T(8,128)(2,1)S(1)} collective-permute-done((bf16[2,1024,256]{2,1,0:T(8,128)(2,1)S(1)}, bf16[2,1024,256]{2,1,0:T(8,128)(2,1)S(1)}, u32[]{:S(2)}, u32[]{:S(2)}) %collective-permute-start.16) | collective-permute-done | bytes 1048608 | tf_op jit(solution)/shard_map/ppermute | solution.py:18
  185.6 6.9 %collective-permute-done.17 = bf16[2,512,256]{2,1,0:T(8,128)(2,1)S(1)} collective-permute-done((bf16[2,512,256]{2,1,0:T(8,128)(2,1)S(1)}, bf16[2,512,256]{2,1,0:T(8,128)(2,1)S(1)}, u32[]{:S(2)}, u32[]{:S(2)}) %collective-permute-start.17) | collective-permute-done | bytes 524320 | tf_op jit(solution)/shard_map/ppermute | solution.py:18
  193.5 3.5 %collective-permute-start.18 = (bf16[2,256,256]{2,1,0:T(8,128)(2,1)}, bf16[2,256,256]{2,1,0:T(8,128)(2,1)S(1)}, u32[]{:S(2)}, u32[]{:S(2)}) collective-permute-start(bf16[2,256,256]{2,1,0:T(8,128)(2,1)} %fusion.51), channel_id=1, source_target_pairs={{0,2},{2,0},{1,3},{3,1},{4,6},{6,4},{5,7},{7,5},{8,10},{10,8},{9,1... | collective-permute-start | bytes 786440 | tf_op jit(solution)/shard_map/ppermute | solution.py:18
  199.1 63.0 %psum.7 = f32[256]{0:T(256)} all-reduce(f32[256]{0:T(256)S(1)} %bitcast.569), channel_id=1, replica_groups=mesh['dp'=8,'ctx'=16] {'dp','ctx'}, use_global_device_ids=true, to_apply=%region_1.2 | all-reduce | flops 256 | bytes 2048 | tf_op jit(solution)/shard_map/psum | solution.py:217
  264.4 3.2 %collective-permute-done.19 = bf16[2,128,256]{2,1,0:T(8,128)(2,1)S(1)} collective-permute-done((bf16[2,128,256]{2,1,0:T(8,128)(2,1)S(1)}, bf16[2,128,256]{2,1,0:T(8,128)(2,1)S(1)}, u32[]{:S(2)}, u32[]{:S(2)}) %collective-permute-start.19) | collective-permute-done | bytes 131104 | tf_op jit(solution)/shard_map/ppermute | solution.py:18
  267.9 2.4 fusion.3
  (328 shorter events, 69.6 us)
Async XLA Ops:
  5.4 26.5 %collective-permute-start = (bf16[2,128,256]{2,1,0:T(8,128)(2,1)S(1)}, bf16[2,128,256]{2,1,0:T(8,128)(2,1)S(1)}, u32[]{:S(2)}, u32[]{:S(2)}) collective-permute-start(bf16[2,128,256]{2,1,0:T(8,128)(2,1)S(1)} %bitcast_dynamic-update-slice_fusion.6), channel_id=1, source_target_pairs={{0,1},{1,0},{2,3},{3,2},{4,5},{5,4},{6,7},{7,6},{8,9},{9,8},{10,11... | collective-permute-start | bytes 393224 | tf_op jit(solution)/shard_map/ppermute | solution.py:18
  7.9 26.5 %collective-permute-start.1 = (bf16[2,128,256]{2,1,0:T(8,128)(2,1)S(1)}, bf16[2,128,256]{2,1,0:T(8,128)(2,1)S(1)}, u32[]{:S(2)}, u32[]{:S(2)}) collective-permute-start(bf16[2,128,256]{2,1,0:T(8,128)(2,1)S(1)} %bitcast_dynamic-update-slice_fusion.4), channel_id=1, source_target_pairs={{0,1},{1,0},{2,3},{3,2},{4,5},{5,4},{6,7},{7,6},{8,9},{9,8},{10,11... | collective-permute-start | bytes 393224 | tf_op jit(solution)/shard_map/ppermute | solution.py:18
  9.4 32.7 %collective-permute-start.3 = (bf16[2,128,256]{2,1,0:T(8,128)(2,1)S(1)}, bf16[2,128,256]{2,1,0:T(8,128)(2,1)S(1)}, u32[]{:S(2)}, u32[]{:S(2)}) collective-permute-start(bf16[2,128,256]{2,1,0:T(8,128)(2,1)S(1)} %bitcast_dynamic-update-slice_fusion.2), channel_id=1, source_target_pairs={{0,1},{1,0},{2,3},{3,2},{4,5},{5,4},{6,7},{7,6},{8,9},{9,8},{10,11... | collective-permute-start | bytes 393224 | tf_op jit(solution)/shard_map/ppermute | solution.py:18
  11.9 27.4 %collective-permute-start.6 = (bf16[2,128,256]{2,1,0:T(8,128)(2,1)S(1)}, bf16[2,128,256]{2,1,0:T(8,128)(2,1)S(1)}, u32[]{:S(2)}, u32[]{:S(2)}) collective-permute-start(bf16[2,128,256]{2,1,0:T(8,128)(2,1)S(1)} %bitcast_dynamic-update-slice_fusion), channel_id=1, source_target_pairs={{0,1},{1,0},{2,3},{3,2},{4,5},{5,4},{6,7},{7,6},{8,9},{9,8},{10,11... | collective-permute-start | bytes 393224 | tf_op jit(solution)/shard_map/ppermute | solution.py:18
  33.0 12.7 %copy-start.61 = (f32[2,1,128]{2,1,0:T(1,128)S(1)}, f32[2,1,128]{2,1,0:T(1,128)}, u32[]{:S(2)}) copy-start(f32[2,1,128]{2,1,0:T(1,128)} %fusion.187) | copy-start | bytes 3076
  34.6 10.8 %collective-permute-start.2 = (bf16[2,256,256]{2,1,0:T(8,128)(2,1)S(1)}, bf16[2,256,256]{2,1,0:T(8,128)(2,1)S(1)}, u32[]{:S(2)}, u32[]{:S(2)}) collective-permute-start(bf16[2,256,256]{2,1,0:T(8,128)(2,1)S(1)} %maximum_select_fusion.7), channel_id=1, source_target_pairs={{0,2},{2,0},{1,3},{3,1},{4,6},{6,4},{5,7},{7,5},{8,10},{10,8},{9,1... | collective-permute-start | bytes 786440 | tf_op jit(solution)/shard_map/ppermute | solution.py:18
  38.7 58.8 %collective-permute-start.10 = (bf16[2,128,256]{2,1,0:T(8,128)(2,1)}, bf16[2,128,256]{2,1,0:T(8,128)(2,1)}, u32[]{:S(2)}, u32[]{:S(2)}) collective-permute-start(bf16[2,128,256]{2,1,0:T(8,128)(2,1)} %fusion.67), channel_id=1, source_target_pairs={{0,1},{1,0},{2,3},{3,2},{4,5},{5,4},{6,7},{7,6},{8,9},{9,8},{10,11... | collective-permute-start | bytes 393224 | tf_op jit(solution)/shard_map/ppermute | solution.py:18
  40.1 26.1 %collective-permute-start.7 = (bf16[2,256,256]{2,1,0:T(8,128)(2,1)}, bf16[2,256,256]{2,1,0:T(8,128)(2,1)}, u32[]{:S(2)}, u32[]{:S(2)}) collective-permute-start(bf16[2,256,256]{2,1,0:T(8,128)(2,1)} %maximum_select_fusion.9), channel_id=1, source_target_pairs={{0,2},{2,0},{1,3},{3,1},{4,6},{6,4},{5,7},{7,5},{8,10},{10,8},{9,1... | collective-permute-start | bytes 786440 | tf_op jit(solution)/shard_map/ppermute | solution.py:18
  42.9 14.2 %collective-permute-start.4 = (bf16[2,256,256]{2,1,0:T(8,128)(2,1)}, bf16[2,256,256]{2,1,0:T(8,128)(2,1)}, u32[]{:S(2)}, u32[]{:S(2)}) collective-permute-start(bf16[2,256,256]{2,1,0:T(8,128)(2,1)} %maximum_select_fusion.8), channel_id=1, source_target_pairs={{0,2},{2,0},{1,3},{3,1},{4,6},{6,4},{5,7},{7,5},{8,10},{10,8},{9,1... | collective-permute-start | bytes 786440 | tf_op jit(solution)/shard_map/ppermute | solution.py:18
  58.4 14.8 %collective-permute-start.5 = (bf16[2,512,256]{2,1,0:T(8,128)(2,1)S(1)}, bf16[2,512,256]{2,1,0:T(8,128)(2,1)}, u32[]{:S(2)}, u32[]{:S(2)}) collective-permute-start(bf16[2,512,256]{2,1,0:T(8,128)(2,1)S(1)} %maximum_select_fusion.4), channel_id=1, source_target_pairs={{0,4},{4,0},{1,5},{5,1},{2,6},{6,2},{3,7},{7,3},{8,12},{12,8},{9,1... | collective-permute-start | bytes 1572872 | tf_op jit(solution)/shard_map/ppermute | solution.py:18
  62.3 12.3 %copy-start.19 = (bf16[2,1,16384]{2,0,1:T(2,128)(2,1)S(1)}, bf16[2,1,16384]{2,0,1:T(2,128)(2,1)}, u32[]{:S(2)}) copy-start(bf16[2,1,16384]{2,0,1:T(2,128)(2,1)} %copy.384) | copy-start | bytes 196612
  63.1 36.2 %collective-permute-start.11 = (bf16[2,256,256]{2,1,0:T(8,128)(2,1)}, bf16[2,256,256]{2,1,0:T(8,128)(2,1)}, u32[]{:S(2)}, u32[]{:S(2)}) collective-permute-start(bf16[2,256,256]{2,1,0:T(8,128)(2,1)} %fusion.49), channel_id=1, source_target_pairs={{0,2},{2,0},{1,3},{3,1},{4,6},{6,4},{5,7},{7,5},{8,10},{10,8},{9,1... | collective-permute-start | bytes 786440 | tf_op jit(solution)/shard_map/ppermute | solution.py:18
  68.3 23.8 %collective-permute-start.8 = (bf16[2,512,256]{2,1,0:T(8,128)(2,1)}, bf16[2,512,256]{2,1,0:T(8,128)(2,1)}, u32[]{:S(2)}, u32[]{:S(2)}) collective-permute-start(bf16[2,512,256]{2,1,0:T(8,128)(2,1)} %maximum_select_fusion.5), channel_id=1, source_target_pairs={{0,4},{4,0},{1,5},{5,1},{2,6},{6,2},{3,7},{7,3},{8,12},{12,8},{9,1... | collective-permute-start | bytes 1572872 | tf_op jit(solution)/shard_map/ppermute | solution.py:18
  89.4 15.5 %collective-permute-start.13 = (bf16[2,512,256]{2,1,0:T(8,128)(2,1)S(1)}, bf16[2,512,256]{2,1,0:T(8,128)(2,1)S(1)}, u32[]{:S(2)}, u32[]{:S(2)}) collective-permute-start(bf16[2,512,256]{2,1,0:T(8,128)(2,1)S(1)} %fusion.42), channel_id=1, source_target_pairs={{0,4},{4,0},{1,5},{5,1},{2,6},{6,2},{3,7},{7,3},{8,12},{12,8},{9,1... | collective-permute-start | bytes 1572872 | tf_op jit(solution)/shard_map/ppermute | solution.py:18
  93.8 29.7 %collective-permute-start.9 = (bf16[2,1024,256]{2,1,0:T(8,128)(2,1)S(1)}, bf16[2,1024,256]{2,1,0:T(8,128)(2,1)S(1)}, u32[]{:S(2)}, u32[]{:S(2)}) collective-permute-start(bf16[2,1024,256]{2,1,0:T(8,128)(2,1)S(1)} %maximum_select_fusion.2), channel_id=1, source_target_pairs={{0,8},{8,0},{1,9},{9,1},{2,10},{10,2},{3,11},{11,3},{4,12},{12,4},... | collective-permute-start | bytes 3145736 | tf_op jit(solution)/shard_map/ppermute | solution.py:18
  101.1 60.6 %collective-permute-start.12 = (bf16[2,128,256]{2,1,0:T(8,128)(2,1)}, bf16[2,128,256]{2,1,0:T(8,128)(2,1)}, u32[]{:S(2)}, u32[]{:S(2)}) collective-permute-start(bf16[2,128,256]{2,1,0:T(8,128)(2,1)} %fusion.68), channel_id=1, source_target_pairs={{0,1},{1,0},{2,3},{3,2},{4,5},{5,4},{6,7},{7,6},{8,9},{9,8},{10,11... | collective-permute-start | bytes 393224 | tf_op jit(solution)/shard_map/ppermute | solution.py:18
  105.1 19.0 %copy-start.18 = (bf16[2,1,16384]{2,0,1:T(2,128)(2,1)S(1)}, bf16[2,1,16384]{2,0,1:T(2,128)(2,1)}, u32[]{:S(2)}) copy-start(bf16[2,1,16384]{2,0,1:T(2,128)(2,1)} %copy.388) | copy-start | bytes 196612
  105.1 19.0 %copy-start.48 = (f32[2]{0:T(128)S(1)}, f32[2]{0:T(128)}, u32[]{:S(2)}) copy-start(f32[2]{0:T(128)} %copy-done.47) | copy-start | bytes 28
  105.2 19.0 %copy-start.59 = (f32[2,1,128]{2,1,0:T(1,128)S(1)}, f32[2,1,128]{2,1,0:T(1,128)}, u32[]{:S(2)}) copy-start(f32[2,1,128]{2,1,0:T(1,128)} %fusion.167) | copy-start | bytes 3076
  158.1 24.7 %collective-permute-start.16 = (bf16[2,1024,256]{2,1,0:T(8,128)(2,1)S(1)}, bf16[2,1024,256]{2,1,0:T(8,128)(2,1)S(1)}, u32[]{:S(2)}, u32[]{:S(2)}) collective-permute-start(bf16[2,1024,256]{2,1,0:T(8,128)(2,1)S(1)} %fusion.36), channel_id=1, source_target_pairs={{0,8},{8,0},{1,9},{9,1},{2,10},{10,2},{3,11},{11,3},{4,12},{12,4},... | collective-permute-start | bytes 3145736 | tf_op jit(solution)/shard_map/ppermute | solution.py:18
  158.3 8.7 %collective-permute-start.14 = (bf16[2,256,256]{2,1,0:T(8,128)(2,1)S(1)}, bf16[2,256,256]{2,1,0:T(8,128)(2,1)S(1)}, u32[]{:S(2)}, u32[]{:S(2)}) collective-permute-start(bf16[2,256,256]{2,1,0:T(8,128)(2,1)S(1)} %fusion.50), channel_id=1, source_target_pairs={{0,2},{2,0},{1,3},{3,1},{4,6},{6,4},{5,7},{7,5},{8,10},{10,8},{9,1... | collective-permute-start | bytes 786440 | tf_op jit(solution)/shard_map/ppermute | solution.py:18
  161.6 21.2 %copy-start = (f32[2,1,1024,256]{3,2,0,1:T(8,128)S(1)}, f32[2,1,1024,256]{3,2,0,1:T(8,128)}, u32[]{:S(2)}) copy-start(f32[2,1,1024,256]{3,2,0,1:T(8,128)} %copy.158) | copy-start | bytes 6291460
  167.1 16.3 %copy-start.12 = (bf16[2,1024,256]{2,1,0:T(8,128)(2,1)S(1)}, bf16[2,1024,256]{2,1,0:T(8,128)(2,1)}, u32[]{:S(2)}) copy-start(bf16[2,1024,256]{2,1,0:T(8,128)(2,1)} %copy-done.11) | copy-start | bytes 3145732
  167.1 16.3 %copy-start.16 = (bf16[2,128,1024]{2,1,0:T(8,128)(2,1)S(1)}, bf16[2,128,1024]{2,1,0:T(8,128)(2,1)}, u32[]{:S(2)}) copy-start(bf16[2,128,1024]{2,1,0:T(8,128)(2,1)} %copy-done.15) | copy-start | bytes 1572868
  167.1 16.7 %collective-permute-start.15 = (bf16[2,128,256]{2,1,0:T(8,128)(2,1)S(1)}, bf16[2,128,256]{2,1,0:T(8,128)(2,1)S(1)}, u32[]{:S(2)}, u32[]{:S(2)}) collective-permute-start(bf16[2,128,256]{2,1,0:T(8,128)(2,1)S(1)} %fusion.69), channel_id=1, source_target_pairs={{0,1},{1,0},{2,3},{3,2},{4,5},{5,4},{6,7},{7,6},{8,9},{9,8},{10,11... | collective-permute-start | bytes 393224 | tf_op jit(solution)/shard_map/ppermute | solution.py:18
  183.3 9.3 %collective-permute-start.17 = (bf16[2,512,256]{2,1,0:T(8,128)(2,1)S(1)}, bf16[2,512,256]{2,1,0:T(8,128)(2,1)S(1)}, u32[]{:S(2)}, u32[]{:S(2)}) collective-permute-start(bf16[2,512,256]{2,1,0:T(8,128)(2,1)S(1)} %fusion.43), channel_id=1, source_target_pairs={{0,4},{4,0},{1,5},{5,1},{2,6},{6,2},{3,7},{7,3},{8,12},{12,8},{9,1... | collective-permute-start | bytes 1572872 | tf_op jit(solution)/shard_map/ppermute | solution.py:18
  193.5 68.7 %collective-permute-start.18 = (bf16[2,256,256]{2,1,0:T(8,128)(2,1)}, bf16[2,256,256]{2,1,0:T(8,128)(2,1)S(1)}, u32[]{:S(2)}, u32[]{:S(2)}) collective-permute-start(bf16[2,256,256]{2,1,0:T(8,128)(2,1)} %fusion.51), channel_id=1, source_target_pairs={{0,2},{2,0},{1,3},{3,1},{4,6},{6,4},{5,7},{7,5},{8,10},{10,8},{9,1... | collective-permute-start | bytes 786440 | tf_op jit(solution)/shard_map/ppermute | solution.py:18
  198.3 65.4 %copy-start.37 = (f32[256]{0:T(256)S(1)}, f32[256]{0:T(256)}, u32[]{:S(2)}) copy-start(f32[256]{0:T(256)} %param.13) | copy-start | bytes 3076
  199.1 68.8 %copy-start.17 = (f32[2,2,32768]{2,1,0:T(2,128)S(1)}, f32[2,2,32768]{2,1,0:T(2,128)}, u32[]{:S(2)}) copy-start(f32[2,2,32768]{2,1,0:T(2,128)} %reshape.1667) | copy-start | bytes 1572868
  199.1 68.8 %copy-start.21 = (f32[1,2,128,256]{3,1,2,0:T(2,128)S(1)}, f32[1,2,128,256]{3,1,2,0:T(2,128)}, u32[]{:S(2)}) copy-start(f32[1,2,128,256]{3,1,2,0:T(2,128)} %copy.191) | copy-start | bytes 786436
  199.1 68.8 %copy-start.22 = (f32[1,2,128,256]{3,1,2,0:T(2,128)S(1)}, f32[1,2,128,256]{3,1,2,0:T(2,128)}, u32[]{:S(2)}) copy-start(f32[1,2,128,256]{3,1,2,0:T(2,128)} %copy.192) | copy-start | bytes 786436
  262.3 5.3 %collective-permute-start.19 = (bf16[2,128,256]{2,1,0:T(8,128)(2,1)S(1)}, bf16[2,128,256]{2,1,0:T(8,128)(2,1)S(1)}, u32[]{:S(2)}, u32[]{:S(2)}) collective-permute-start(bf16[2,128,256]{2,1,0:T(8,128)(2,1)S(1)} %fusion.70), channel_id=1, source_target_pairs={{0,1},{1,0},{2,3},{3,2},{4,5},{5,4},{6,7},{7,6},{8,9},{9,8},{10,11... | collective-permute-start | bytes 393224 | tf_op jit(solution)/shard_map/ppermute | solution.py:18
  (51 other events, 309.8 us)
where the time goes:
time: 277 us; the launch traced here: 273 us
  waiting for transfers between devices  63.6 us (23%)
  blocking collectives  63 us (23%)
  local copies, waits for them, and re-layouts  59.3 us (21%)
  starting transfers between devices  34.9 us (13%)
  other arithmetic  27.5 us (10%)
  matrix products  21.6 us (8%)
    ppermute x20, waiting for transfers between devices, swapped(): return lax.ppermute(block, axis, route)  63.6 us
    psum x1, blocking collectives, body(): lax.psum(jnp.sum(query_raw.astype(jnp.float32) * dq_rows, axis=0), ('dp',...  63 us
    ppermute x20, starting transfers between devices, swapped(): return lax.ppermute(block, axis, route)  34.9 us
    unnamed x153, local copies, waits for them, and re-layouts  24.8 us
    slice x3, local copies, waits for them, and re-layouts, swap_down(): kept_half = jnp.where(lower_half, halves[:, 0], halves[:, 1])  12.9 us
    reshape x3, local copies, waits for them, and re-layouts, swap_down(): halves = sums_kv.reshape(head_count, 2, -1, sums_kv.shape[-1])  10.3 us
    dot_general x25, matrix products, pick_blocks(): jnp.einsum('hsb,hbx->hsx', table, flat, precision=lax.Precision.HIGHEST,...  10.3 us
    select_n x10, other arithmetic, swap_up(): jnp.where(lower_half, jnp.concatenate([payload, partner], axis=1), jnp.co...  9.27 us
  transfers between devices with their start and end apart: 20, of which 9 were waited for; matrix products, arithmetic and copies ran while one was open for 34% of the time, Pallas kernels for 0%

commit v1 on v0

--- a/solution.py
+++ b/solution.py
@@ -214,7 +214,10 @@
     grad_queries = (dq_rows * q_gain).astype(jnp.bfloat16)
     grad_keys = to_rows(kv_acc[..., :head_dim]).astype(jnp.bfloat16)
     grad_values = to_rows(kv_acc[..., head_dim:]).astype(jnp.bfloat16)
-    gain_total = lax.psum(jnp.sum(query_raw.astype(jnp.float32) * dq_rows, axis=0), ("dp", "ctx"))
+    gain_total = jnp.sum(
+        lax.all_gather(jnp.sum(query_raw.astype(jnp.float32) * dq_rows, axis=0), ("dp", "ctx")),
+        axis=0,
+    )
     return (grad_queries[None], grad_keys[None], grad_values[None], gain_total)
 
 

time: 277 us -> 265 us (0.957)
  the two profiles are of different devices: /device:TPU:0 before, /device:TPU:1 now
where the time goes in v1:
time: 265 us; the launch traced here: 260 us
  blocking collectives  61.7 us (23%)
  local copies, waits for them, and re-layouts  59.1 us (22%)
  waiting for transfers between devices  56.8 us (21%)
  starting transfers between devices  29.3 us (11%)
  other arithmetic  29.2 us (11%)
  matrix products  21.7 us (8%)
    all_gather x1, blocking collectives, body(): lax.all_gather(jnp.sum(query_raw.astype(jnp.float32) * dq_rows, axis=0),...  61.7 us
    ppermute x20, waiting for transfers between devices, swapped(): return lax.ppermute(block, axis, route)  56.8 us
    ppermute x20, starting transfers between devices, swapped(): return lax.ppermute(block, axis, route)  29.3 us
    unnamed x153, local copies, waits for them, and re-layouts  24.6 us
    slice x3, local copies, waits for them, and re-layouts, swap_down(): kept_half = jnp.where(lower_half, halves[:, 0], halves[:, 1])  12.9 us
    reshape x3, local copies, waits for them, and re-layouts, swap_down(): halves = sums_kv.reshape(head_count, 2, -1, sums_kv.shape[-1])  10.3 us
    dot_general x25, matrix products, pick_blocks(): jnp.einsum('hsb,hbx->hsx', table, flat, precision=lax.Precision.HIGHEST,...  10.3 us
    select_n x10, other arithmetic, swap_up(): jnp.where(lower_half, jnp.concatenate([payload, partner], axis=1), jnp.co...  9.28 us
  transfers between devices with their start and end apart: 20, of which 7 were waited for; matrix products, arithmetic and copies ran while one was open for 36% of the time, Pallas kernels for 0%

profile of v1, /device:TPU:1, one launch (start us, length us, event | category | flops | bytes accessed | tf_op | source)
XLA Modules:
  0.0 260.3 jit_solution(7653714906080200234)
XLA Ops:
  1.7 1.7 clamp_reduce_fusion.3
  5.4 2.1 collective-permute-start
  9.4 1.5 collective-permute-start.3
  34.1 3.0 %collective-permute-start.2 = (bf16[2,256,256]{2,1,0:T(8,128)(2,1)S(1)}, bf16[2,256,256]{2,1,0:T(8,128)(2,1)S(1)}, u32[]{:S(2)}, u32[]{:S(2)}) collective-permute-start(bf16[2,256,256]{2,1,0:T(8,128)(2,1)S(1)} %maximum_select_fusion.7), channel_id=1, source_target_pairs={{0,2},{2,0},{1,3},{3,1},{4,6},{6,4},{5,7},{7,5},{8,10},{10,8},{9,1... | collective-permute-start | bytes 786440 | tf_op jit(solution)/shard_map/ppermute | solution.py:18
  39.1 1.7 collective-permute-start.7
  45.5 10.2 %collective-permute-done.4 = bf16[2,256,256]{2,1,0:T(8,128)(2,1)} collective-permute-done((bf16[2,256,256]{2,1,0:T(8,128)(2,1)}, bf16[2,256,256]{2,1,0:T(8,128)(2,1)}, u32[]{:S(2)}, u32[]{:S(2)}) %collective-permute-start.4) | collective-permute-done | bytes 262176 | tf_op jit(solution)/shard_map/ppermute | solution.py:18
  57.0 2.2 collective-permute-start.5
  61.5 2.7 %collective-permute-start.11 = (bf16[2,256,256]{2,1,0:T(8,128)(2,1)}, bf16[2,256,256]{2,1,0:T(8,128)(2,1)}, u32[]{:S(2)}, u32[]{:S(2)}) collective-permute-start(bf16[2,256,256]{2,1,0:T(8,128)(2,1)} %fusion.49), channel_id=1, source_target_pairs={{0,2},{2,0},{1,3},{3,1},{4,6},{6,4},{5,7},{7,5},{8,10},{10,8},{9,1... | collective-permute-start | bytes 786440 | tf_op jit(solution)/shard_map/ppermute | solution.py:18
  64.3 2.2 maximum_select_fusion.5
  66.5 2.4 collective-permute-done.5
  72.7 1.5 pad_maximum_fusion.1
  74.2 3.0 %reshape.1674 = f32[2,2,512,256]{2,1,3,0:T(2,128)S(1)} reshape(f32[2,1024,256]{1,2,0:T(8,128)} %pad_maximum_fusion.1) | data formatting | bytes 4194304 | tf_op jit(solution)/shard_map/reshape | solution.py:137
  77.2 2.9 %fusion.212 = (f32[2,1,512,256]{2,1,3,0:T(1,128)}, f32[2,1,512,256]{2,1,3,0:T(1,128)}) fusion(f32[2,2,512,256]{2,1,3,0:T(2,128)S(1)} %reshape.1674), kind=kLoop, calls=%fused_computation.413 | loop fusion | bytes 4194304 | tf_op jit(solution)/shard_map/slice | solution.py:139
  80.2 2.3 copy.200
  82.5 2.4 copy.201
  86.3 1.8 maximum_select_fusion.2
  88.1 3.4 %collective-permute-start.9 = (bf16[2,1024,256]{2,1,0:T(8,128)(2,1)S(1)}, bf16[2,1024,256]{2,1,0:T(8,128)(2,1)S(1)}, u32[]{:S(2)}, u32[]{:S(2)}) collective-permute-start(bf16[2,1024,256]{2,1,0:T(8,128)(2,1)S(1)} %maximum_select_fusion.2), channel_id=1, source_target_pairs={{0,8},{8,0},{1,9},{9,1},{2,10},{10,2},{3,11},{11,3},{4,12},{12,4},... | collective-permute-start | bytes 3145736 | tf_op jit(solution)/shard_map/ppermute | solution.py:18
  96.8 20.4 %collective-permute-done.9 = bf16[2,1024,256]{2,1,0:T(8,128)(2,1)S(1)} collective-permute-done((bf16[2,1024,256]{2,1,0:T(8,128)(2,1)S(1)}, bf16[2,1024,256]{2,1,0:T(8,128)(2,1)S(1)}, u32[]{:S(2)}, u32[]{:S(2)}) %collective-permute-start.9) | collective-permute-done | bytes 1048608 | tf_op jit(solution)/shard_map/ppermute | solution.py:18
  121.1 2.5 pad_maximum_fusion
  123.6 6.6 %reshape.1678 = f32[2,2,1024,256]{2,1,3,0:T(2,128)} reshape(f32[2,2048,256]{1,2,0:T(8,128)} %pad_maximum_fusion) | data formatting | bytes 8388608 | tf_op jit(solution)/shard_map/reshape | solution.py:137
  130.2 9.1 %fusion.211 = (f32[2,1,1024,256]{2,1,3,0:T(1,128)}, f32[2,1,1024,256]{2,1,3,0:T(1,128)}) fusion(f32[2,2,1024,256]{2,1,3,0:T(2,128)} %reshape.1678), kind=kLoop, calls=%fused_computation.412 | loop fusion | bytes 8388608 | tf_op jit(solution)/shard_map/slice | solution.py:139
  139.3 4.6 %copy.206 = f32[2,1,1024,256]{3,2,0,1:T(8,128)S(1)} copy(f32[2,1,1024,256]{2,1,3,0:T(1,128)} %get-tuple-element.141) | data formatting | bytes 4194304
  143.8 6.0 %copy.207 = f32[2,1,1024,256]{3,2,0,1:T(8,128)} copy(f32[2,1,1024,256]{2,1,3,0:T(1,128)} %get-tuple-element.142) | data formatting | bytes 4194304
  149.9 1.9 fusion.36
  151.9 2.8 %collective-permute-start.14 = (bf16[2,256,256]{2,1,0:T(8,128)(2,1)S(1)}, bf16[2,256,256]{2,1,0:T(8,128)(2,1)S(1)}, u32[]{:S(2)}, u32[]{:S(2)}) collective-permute-start(bf16[2,256,256]{2,1,0:T(8,128)(2,1)S(1)} %fusion.50), channel_id=1, source_target_pairs={{0,2},{2,0},{1,3},{3,1},{4,6},{6,4},{5,7},{7,5},{8,10},{10,8},{9,1... | collective-permute-start | bytes 786440 | tf_op jit(solution)/shard_map/ppermute | solution.py:18
  157.0 1.7 collective-permute-done.14
  160.1 10.1 %collective-permute-done.16 = bf16[2,1024,256]{2,1,0:T(8,128)(2,1)S(1)} collective-permute-done((bf16[2,1024,256]{2,1,0:T(8,128)(2,1)S(1)}, bf16[2,1024,256]{2,1,0:T(8,128)(2,1)S(1)}, u32[]{:S(2)}, u32[]{:S(2)}) %collective-permute-start.16) | collective-permute-done | bytes 1048608 | tf_op jit(solution)/shard_map/ppermute | solution.py:18
  173.1 8.0 %collective-permute-done.17 = bf16[2,512,256]{2,1,0:T(8,128)(2,1)S(1)} collective-permute-done((bf16[2,512,256]{2,1,0:T(8,128)(2,1)S(1)}, bf16[2,512,256]{2,1,0:T(8,128)(2,1)S(1)}, u32[]{:S(2)}, u32[]{:S(2)}) %collective-permute-start.17) | collective-permute-done | bytes 524320 | tf_op jit(solution)/shard_map/ppermute | solution.py:18
  182.0 2.6 collective-permute-start.18
  186.6 61.7 %all-gather = f32[128,1,256]{2,1,0:T(1,128)S(1)} all-gather(f32[1,1,256]{2,1,0:T(1,128)S(1)} %bitcast.569), channel_id=1, replica_groups=mesh['dp'=8,'ctx'=16] {'dp','ctx'}, dimensions={0}, use_global_device_ids=true | all-gather | bytes 132096 | tf_op jit(solution)/shard_map/all_gather | solution.py:218
  251.4 3.9 %collective-permute-done.19 = bf16[2,128,256]{2,1,0:T(8,128)(2,1)S(1)} collective-permute-done((bf16[2,128,256]{2,1,0:T(8,128)(2,1)S(1)}, bf16[2,128,256]{2,1,0:T(8,128)(2,1)S(1)}, u32[]{:S(2)}, u32[]{:S(2)}) %collective-permute-start.19) | collective-permute-done | bytes 131104 | tf_op jit(solution)/shard_map/ppermute | solution.py:18
  255.6 2.4 fusion.3
  (329 shorter events, 66.2 us)
Async XLA Ops:
  5.4 26.0 %collective-permute-start = (bf16[2,128,256]{2,1,0:T(8,128)(2,1)S(1)}, bf16[2,128,256]{2,1,0:T(8,128)(2,1)S(1)}, u32[]{:S(2)}, u32[]{:S(2)}) collective-permute-start(bf16[2,128,256]{2,1,0:T(8,128)(2,1)S(1)} %bitcast_dynamic-update-slice_fusion.6), channel_id=1, source_target_pairs={{0,1},{1,0},{2,3},{3,2},{4,5},{5,4},{6,7},{7,6},{8,9},{9,8},{10,11... | collective-permute-start | bytes 393224 | tf_op jit(solution)/shard_map/ppermute | solution.py:18
  8.4 25.6 %collective-permute-start.1 = (bf16[2,128,256]{2,1,0:T(8,128)(2,1)S(1)}, bf16[2,128,256]{2,1,0:T(8,128)(2,1)S(1)}, u32[]{:S(2)}, u32[]{:S(2)}) collective-permute-start(bf16[2,128,256]{2,1,0:T(8,128)(2,1)S(1)} %bitcast_dynamic-update-slice_fusion.4), channel_id=1, source_target_pairs={{0,1},{1,0},{2,3},{3,2},{4,5},{5,4},{6,7},{7,6},{8,9},{9,8},{10,11... | collective-permute-start | bytes 393224 | tf_op jit(solution)/shard_map/ppermute | solution.py:18
  9.4 31.4 %collective-permute-start.3 = (bf16[2,128,256]{2,1,0:T(8,128)(2,1)S(1)}, bf16[2,128,256]{2,1,0:T(8,128)(2,1)S(1)}, u32[]{:S(2)}, u32[]{:S(2)}) collective-permute-start(bf16[2,128,256]{2,1,0:T(8,128)(2,1)S(1)} %bitcast_dynamic-update-slice_fusion.2), channel_id=1, source_target_pairs={{0,1},{1,0},{2,3},{3,2},{4,5},{5,4},{6,7},{7,6},{8,9},{9,8},{10,11... | collective-permute-start | bytes 393224 | tf_op jit(solution)/shard_map/ppermute | solution.py:18
  11.8 26.5 %collective-permute-start.6 = (bf16[2,128,256]{2,1,0:T(8,128)(2,1)S(1)}, bf16[2,128,256]{2,1,0:T(8,128)(2,1)S(1)}, u32[]{:S(2)}, u32[]{:S(2)}) collective-permute-start(bf16[2,128,256]{2,1,0:T(8,128)(2,1)S(1)} %bitcast_dynamic-update-slice_fusion), channel_id=1, source_target_pairs={{0,1},{1,0},{2,3},{3,2},{4,5},{5,4},{6,7},{7,6},{8,9},{9,8},{10,11... | collective-permute-start | bytes 393224 | tf_op jit(solution)/shard_map/ppermute | solution.py:18
  34.1 8.9 %collective-permute-start.2 = (bf16[2,256,256]{2,1,0:T(8,128)(2,1)S(1)}, bf16[2,256,256]{2,1,0:T(8,128)(2,1)S(1)}, u32[]{:S(2)}, u32[]{:S(2)}) collective-permute-start(bf16[2,256,256]{2,1,0:T(8,128)(2,1)S(1)} %maximum_select_fusion.7), channel_id=1, source_target_pairs={{0,2},{2,0},{1,3},{3,1},{4,6},{6,4},{5,7},{7,5},{8,10},{10,8},{9,1... | collective-permute-start | bytes 786440 | tf_op jit(solution)/shard_map/ppermute | solution.py:18
  38.0 53.5 %collective-permute-start.10 = (bf16[2,128,256]{2,1,0:T(8,128)(2,1)}, bf16[2,128,256]{2,1,0:T(8,128)(2,1)}, u32[]{:S(2)}, u32[]{:S(2)}) collective-permute-start(bf16[2,128,256]{2,1,0:T(8,128)(2,1)} %fusion.67), channel_id=1, source_target_pairs={{0,1},{1,0},{2,3},{3,2},{4,5},{5,4},{6,7},{7,6},{8,9},{9,8},{10,11... | collective-permute-start | bytes 393224 | tf_op jit(solution)/shard_map/ppermute | solution.py:18
  39.1 25.1 %collective-permute-start.7 = (bf16[2,256,256]{2,1,0:T(8,128)(2,1)}, bf16[2,256,256]{2,1,0:T(8,128)(2,1)}, u32[]{:S(2)}, u32[]{:S(2)}) collective-permute-start(bf16[2,256,256]{2,1,0:T(8,128)(2,1)} %maximum_select_fusion.9), channel_id=1, source_target_pairs={{0,2},{2,0},{1,3},{3,1},{4,6},{6,4},{5,7},{7,5},{8,10},{10,8},{9,1... | collective-permute-start | bytes 786440 | tf_op jit(solution)/shard_map/ppermute | solution.py:18
  41.7 13.9 %collective-permute-start.4 = (bf16[2,256,256]{2,1,0:T(8,128)(2,1)}, bf16[2,256,256]{2,1,0:T(8,128)(2,1)}, u32[]{:S(2)}, u32[]{:S(2)}) collective-permute-start(bf16[2,256,256]{2,1,0:T(8,128)(2,1)} %maximum_select_fusion.8), channel_id=1, source_target_pairs={{0,2},{2,0},{1,3},{3,1},{4,6},{6,4},{5,7},{7,5},{8,10},{10,8},{9,1... | collective-permute-start | bytes 786440 | tf_op jit(solution)/shard_map/ppermute | solution.py:18
  57.0 11.9 %collective-permute-start.5 = (bf16[2,512,256]{2,1,0:T(8,128)(2,1)S(1)}, bf16[2,512,256]{2,1,0:T(8,128)(2,1)}, u32[]{:S(2)}, u32[]{:S(2)}) collective-permute-start(bf16[2,512,256]{2,1,0:T(8,128)(2,1)S(1)} %maximum_select_fusion.4), channel_id=1, source_target_pairs={{0,4},{4,0},{1,5},{5,1},{2,6},{6,2},{3,7},{7,3},{8,12},{12,8},{9,1... | collective-permute-start | bytes 1572872 | tf_op jit(solution)/shard_map/ppermute | solution.py:18
  61.5 31.8 %collective-permute-start.11 = (bf16[2,256,256]{2,1,0:T(8,128)(2,1)}, bf16[2,256,256]{2,1,0:T(8,128)(2,1)}, u32[]{:S(2)}, u32[]{:S(2)}) collective-permute-start(bf16[2,256,256]{2,1,0:T(8,128)(2,1)} %fusion.49), channel_id=1, source_target_pairs={{0,2},{2,0},{1,3},{3,1},{4,6},{6,4},{5,7},{7,5},{8,10},{10,8},{9,1... | collective-permute-start | bytes 786440 | tf_op jit(solution)/shard_map/ppermute | solution.py:18
  66.4 19.9 %collective-permute-start.8 = (bf16[2,512,256]{2,1,0:T(8,128)(2,1)}, bf16[2,512,256]{2,1,0:T(8,128)(2,1)}, u32[]{:S(2)}, u32[]{:S(2)}) collective-permute-start(bf16[2,512,256]{2,1,0:T(8,128)(2,1)} %maximum_select_fusion.5), channel_id=1, source_target_pairs={{0,4},{4,0},{1,5},{5,1},{2,6},{6,2},{3,7},{7,3},{8,12},{12,8},{9,1... | collective-permute-start | bytes 1572872 | tf_op jit(solution)/shard_map/ppermute | solution.py:18
  85.1 11.5 %collective-permute-start.13 = (bf16[2,512,256]{2,1,0:T(8,128)(2,1)S(1)}, bf16[2,512,256]{2,1,0:T(8,128)(2,1)S(1)}, u32[]{:S(2)}, u32[]{:S(2)}) collective-permute-start(bf16[2,512,256]{2,1,0:T(8,128)(2,1)S(1)} %fusion.42), channel_id=1, source_target_pairs={{0,4},{4,0},{1,5},{5,1},{2,6},{6,2},{3,7},{7,3},{8,12},{12,8},{9,1... | collective-permute-start | bytes 1572872 | tf_op jit(solution)/shard_map/ppermute | solution.py:18
  88.1 29.1 %collective-permute-start.9 = (bf16[2,1024,256]{2,1,0:T(8,128)(2,1)S(1)}, bf16[2,1024,256]{2,1,0:T(8,128)(2,1)S(1)}, u32[]{:S(2)}, u32[]{:S(2)}) collective-permute-start(bf16[2,1024,256]{2,1,0:T(8,128)(2,1)S(1)} %maximum_select_fusion.2), channel_id=1, source_target_pairs={{0,8},{8,0},{1,9},{9,1},{2,10},{10,2},{3,11},{11,3},{4,12},{12,4},... | collective-permute-start | bytes 3145736 | tf_op jit(solution)/shard_map/ppermute | solution.py:18
  95.1 59.9 %collective-permute-start.12 = (bf16[2,128,256]{2,1,0:T(8,128)(2,1)}, bf16[2,128,256]{2,1,0:T(8,128)(2,1)}, u32[]{:S(2)}, u32[]{:S(2)}) collective-permute-start(bf16[2,128,256]{2,1,0:T(8,128)(2,1)} %fusion.68), channel_id=1, source_target_pairs={{0,1},{1,0},{2,3},{3,2},{4,5},{5,4},{6,7},{7,6},{8,9},{9,8},{10,11... | collective-permute-start | bytes 393224 | tf_op jit(solution)/shard_map/ppermute | solution.py:18
  96.7 21.0 %copy-start.18 = (bf16[2,1,16384]{2,0,1:T(2,128)(2,1)S(1)}, bf16[2,1,16384]{2,0,1:T(2,128)(2,1)}, u32[]{:S(2)}) copy-start(bf16[2,1,16384]{2,0,1:T(2,128)(2,1)} %copy.437) | copy-start | bytes 196612
  96.8 21.0 %copy-start.48 = (f32[2]{0:T(128)S(1)}, f32[2]{0:T(128)}, u32[]{:S(2)}) copy-start(f32[2]{0:T(128)} %copy-done.47) | copy-start | bytes 28
  96.8 21.0 %copy-start.59 = (f32[2,1,128]{2,1,0:T(1,128)S(1)}, f32[2,1,128]{2,1,0:T(1,128)}, u32[]{:S(2)}) copy-start(f32[2,1,128]{2,1,0:T(1,128)} %fusion.167) | copy-start | bytes 3076
  151.8 18.5 %collective-permute-start.16 = (bf16[2,1024,256]{2,1,0:T(8,128)(2,1)S(1)}, bf16[2,1024,256]{2,1,0:T(8,128)(2,1)S(1)}, u32[]{:S(2)}, u32[]{:S(2)}) collective-permute-start(bf16[2,1024,256]{2,1,0:T(8,128)(2,1)S(1)} %fusion.36), channel_id=1, source_target_pairs={{0,8},{8,0},{1,9},{9,1},{2,10},{10,2},{3,11},{11,3},{4,12},{12,4},... | collective-permute-start | bytes 3145736 | tf_op jit(solution)/shard_map/ppermute | solution.py:18
  151.9 6.8 %collective-permute-start.14 = (bf16[2,256,256]{2,1,0:T(8,128)(2,1)S(1)}, bf16[2,256,256]{2,1,0:T(8,128)(2,1)S(1)}, u32[]{:S(2)}, u32[]{:S(2)}) collective-permute-start(bf16[2,256,256]{2,1,0:T(8,128)(2,1)S(1)} %fusion.50), channel_id=1, source_target_pairs={{0,2},{2,0},{1,3},{3,1},{4,6},{6,4},{5,7},{7,5},{8,10},{10,8},{9,1... | collective-permute-start | bytes 786440 | tf_op jit(solution)/shard_map/ppermute | solution.py:18
  154.9 15.3 %copy-start = (f32[2,1,1024,256]{3,2,0,1:T(8,128)S(1)}, f32[2,1,1024,256]{3,2,0,1:T(8,128)}, u32[]{:S(2)}) copy-start(f32[2,1,1024,256]{3,2,0,1:T(8,128)} %copy.207) | copy-start | bytes 6291460
  158.9 12.2 %copy-start.12 = (bf16[2,1024,256]{2,1,0:T(8,128)(2,1)S(1)}, bf16[2,1024,256]{2,1,0:T(8,128)(2,1)}, u32[]{:S(2)}) copy-start(bf16[2,1024,256]{2,1,0:T(8,128)(2,1)} %copy-done.11) | copy-start | bytes 3145732
  158.9 12.2 %copy-start.16 = (bf16[2,128,1024]{2,1,0:T(8,128)(2,1)S(1)}, bf16[2,128,1024]{2,1,0:T(8,128)(2,1)}, u32[]{:S(2)}) copy-start(bf16[2,128,1024]{2,1,0:T(8,128)(2,1)} %copy-done.15) | copy-start | bytes 1572868
  158.9 12.6 %collective-permute-start.15 = (bf16[2,128,256]{2,1,0:T(8,128)(2,1)S(1)}, bf16[2,128,256]{2,1,0:T(8,128)(2,1)S(1)}, u32[]{:S(2)}, u32[]{:S(2)}) collective-permute-start(bf16[2,128,256]{2,1,0:T(8,128)(2,1)S(1)} %fusion.69), channel_id=1, source_target_pairs={{0,1},{1,0},{2,3},{3,2},{4,5},{5,4},{6,7},{7,6},{8,9},{9,8},{10,11... | collective-permute-start | bytes 393224 | tf_op jit(solution)/shard_map/ppermute | solution.py:18
  170.7 10.4 %collective-permute-start.17 = (bf16[2,512,256]{2,1,0:T(8,128)(2,1)S(1)}, bf16[2,512,256]{2,1,0:T(8,128)(2,1)S(1)}, u32[]{:S(2)}, u32[]{:S(2)}) collective-permute-start(bf16[2,512,256]{2,1,0:T(8,128)(2,1)S(1)} %fusion.43), channel_id=1, source_target_pairs={{0,4},{4,0},{1,5},{5,1},{2,6},{6,2},{3,7},{7,3},{8,12},{12,8},{9,1... | collective-permute-start | bytes 1572872 | tf_op jit(solution)/shard_map/ppermute | solution.py:18
  173.0 11.6 %copy-start.20 = (f32[2,2,16384]{2,1,0:T(2,128)S(1)}, f32[2,2,16384]{2,1,0:T(2,128)}, u32[]{:S(2)}) copy-start(f32[2,2,16384]{2,1,0:T(2,128)} %reshape_reshape_transpose.2) | copy-start | bytes 786436
  173.0 11.6 %copy-start.26 = (f32[1,2,128,128]{3,1,2,0:T(2,128)S(1)}, f32[1,2,128,128]{3,1,2,0:T(2,128)}, u32[]{:S(2)}) copy-start(f32[1,2,128,128]{3,1,2,0:T(2,128)} %copy.422) | copy-start | bytes 393220
  173.0 11.6 %copy-start.52 = (f32[2,2]{1,0:T(2,128)S(1)}, f32[2,2]{1,0:T(2,128)}, u32[]{:S(2)}) copy-start(f32[2,2]{1,0:T(2,128)} %copy-done.51) | copy-start | bytes 52
  173.0 11.6 %copy-start.53 = (f32[2,2]{1,0:T(2,128)S(1)}, f32[2,2]{1,0:T(2,128)}, u32[]{:S(2)}) copy-start(f32[2,2]{1,0:T(2,128)} %get-tuple-element.207) | copy-start | bytes 52
  173.1 11.6 %copy-start.54 = (f32[2,2]{1,0:T(2,128)S(1)}, f32[2,2]{1,0:T(2,128)}, u32[]{:S(2)}) copy-start(f32[2,2]{1,0:T(2,128)} %get-tuple-element.208) | copy-start | bytes 52
  182.0 67.0 %collective-permute-start.18 = (bf16[2,256,256]{2,1,0:T(8,128)(2,1)}, bf16[2,256,256]{2,1,0:T(8,128)(2,1)}, u32[]{:S(2)}, u32[]{:S(2)}) collective-permute-start(bf16[2,256,256]{2,1,0:T(8,128)(2,1)} %fusion.51), channel_id=1, source_target_pairs={{0,2},{2,0},{1,3},{3,1},{4,6},{6,4},{5,7},{7,5},{8,10},{10,8},{9,1... | collective-permute-start | bytes 786440 | tf_op jit(solution)/shard_map/ppermute | solution.py:18
  186.1 64.6 %copy-start.37 = (f32[256]{0:T(256)S(1)}, f32[256]{0:T(256)}, u32[]{:S(2)}) copy-start(f32[256]{0:T(256)} %param.13) | copy-start | bytes 3076
  250.1 5.2 %collective-permute-start.19 = (bf16[2,128,256]{2,1,0:T(8,128)(2,1)S(1)}, bf16[2,128,256]{2,1,0:T(8,128)(2,1)S(1)}, u32[]{:S(2)}, u32[]{:S(2)}) collective-permute-start(bf16[2,128,256]{2,1,0:T(8,128)(2,1)S(1)} %fusion.70), channel_id=1, source_target_pairs={{0,1},{1,0},{2,3},{3,2},{4,5},{5,4},{6,7},{7,6},{8,9},{9,8},{10,11... | collective-permute-start | bytes 393224 | tf_op jit(solution)/shard_map/ppermute | solution.py:18
  (51 other events, 282.5 us)
